TPU v7x, 32 devices: a whole 2x2x4 slice. The times are simulated.
32 devices in a mesh: replica: 8 (over y, x, core), tok: 4 (over z).
Axes of the slice: x: 2, y: 2, z: 4, core: 2. Of those that a mesh axis runs over, the one named last changes fastest.
Arguments:
- activations: bfloat16 [8192, 2880], P(('replica', 'tok')), may hold values from -6 to 6
- cotangent: bfloat16 [8192, 512], P(('replica', 'tok')), may hold values from -6 to 6
- next_inputs: bfloat16 [8192, 2880], P(('replica', 'tok')), may hold values from -6 to 6
- weight_tiles: bfloat16 [360, 4096], P('tok'), may hold values from -0.109375 to 0.109375
- momentum: float32 [8, 360, 4096], P('replica', 'tok'), may hold values from -6 to 6
- chosen: int32 [8, 4, 8], P('replica', 'tok'), may hold values from 0 to 89, as said below
- counts: int32 [8, 4], P('replica', 'tok'), may hold values from 1 to 8, as said below
Outputs:
- values: bfloat16 [8192, 512], P(('replica', 'tok'))
- new_momentum: float32 [8, 360, 4096], P('replica', 'tok')
Inputs may be any that keep to these rules, and one draw needn't show every extreme that they name: Each list chosen[r, k] names 8 different tile numbers of the shard's 90 tiles; only the first counts[r, k] of them are selected. `counts`: in every draw some token shard has 8 selected tiles in every replica.
All inputs are finite; a program needn't handle non-finite values.
Results may differ from a plain program's by a relative error of at most 0.015.
Values may be sent and summed in bfloat16 or wider, within the bound.
No kernel may reach another device: no remote copies, remote signals or barrier semaphores. Data moves between devices by JAX's collectives and lax.ppermute only.
A program may use at most 64 MiB of HBM per device.

v0:
```python
import math
import jax
import jax.numpy as jnp
from jax import lax
from jax.sharding import PartitionSpec as P

TILE = 64
KEEP = 32
momentum_decay = 0.9
step_size = 0.01


def cosine_rows(count):
    frequency = jnp.arange(count, dtype=jnp.float32)[:, None]
    position = jnp.arange(TILE, dtype=jnp.float32)[None, :]
    cosines = jnp.cos(math.pi * (2.0 * position + 1.0) * frequency / (2.0 * TILE))
    factor = jnp.where(frequency == 0, math.sqrt(1.0 / TILE), math.sqrt(2.0 / TILE))
    return cosines * factor


def rebuild(summed, weight_part, keep_rows):
    quads = summed.reshape(summed.shape[0], KEEP, KEEP)
    update = jnp.einsum(
        "ua,tuv,vb->tab", keep_rows, quads, keep_rows, precision=lax.Precision.HIGHEST
    )
    shifted = weight_part.astype(jnp.float32) - step_size * update.reshape(
        summed.shape[0], TILE * TILE
    )
    return shifted.astype(jnp.bfloat16)


def forward(inputs, new_tiles):
    row_tiles = inputs.shape[1] // TILE
    col_tiles = new_tiles.shape[0] // row_tiles
    blocks = inputs.reshape(inputs.shape[0], row_tiles, TILE)
    matrix = new_tiles.reshape(row_tiles, col_tiles, TILE, TILE)
    output = jnp.einsum("tra,rcab->tcb", blocks, matrix, preferred_element_type=jnp.float32)
    return output.reshape(inputs.shape[0], col_tiles * TILE).astype(jnp.bfloat16)


def local(activations, cotangent, next_inputs, weight_tiles, momentum, chosen, counts):
    highest = lax.Precision.HIGHEST
    shards = lax.axis_size("tok")
    tiles_here = weight_tiles.shape[0]
    row_tiles = activations.shape[1] // TILE
    col_tiles = cotangent.shape[1] // TILE
    grad_scale = 1.0 / math.sqrt(activations.shape[0] * shards)
    keep_rows = cosine_rows(KEEP)
    row_span = min(tiles_here * lax.axis_size("tok") // col_tiles + 2, row_tiles)
    product = (
        lax.dot_general(
            activations, cotangent, (((0,), (0,)), ((), ())), preferred_element_type=jnp.float32
        )
        * grad_scale
    )
    tiled = product.reshape(row_span, TILE, col_tiles, TILE).transpose(0, 2, 1, 3)
    tiled = tiled.reshape(row_span * col_tiles, TILE * TILE)
    gradient = lax.psum_scatter(
        tiled.astype(jnp.bfloat16), "tok", scatter_dimension=0, tiled=True
    ).astype(jnp.float32)
    updated = momentum_decay * momentum[0] + gradient
    chosen_here = chosen[0, 0]
    in_list = jnp.arange(chosen_here.shape[0], dtype=jnp.int32) < counts[0, 0]
    picked = jnp.take(updated, chosen_here, axis=0).reshape(-1, TILE, TILE)
    quadrant = jnp.einsum("ua,nab,vb->nuv", keep_rows, picked, keep_rows, precision=highest)
    quadrant = jnp.where(in_list[:, None, None], quadrant, 0.0).astype(jnp.bfloat16)
    rebuilt = jnp.einsum(
        "ua,nuv,vb->nab", keep_rows, quadrant.astype(jnp.float32), keep_rows, precision=highest
    )
    new_momentum = updated.at[chosen_here].add(-rebuilt.reshape(-1, TILE * TILE))
    listed = jnp.where(in_list, chosen_here, -1)
    flat_quads = quadrant.reshape(-1, KEEP * KEEP)
    tile_numbers = jnp.arange(tiles_here, dtype=jnp.int32)
    all_quads, all_listed = (
        lax.all_gather(flat_quads, "replica", axis=0, tiled=True),
        lax.all_gather(listed, "replica", axis=0, tiled=True),
    )
    one_hot = (all_listed[:, None] == tile_numbers[None, :]).astype(jnp.bfloat16)
    summed = lax.dot_general(
        one_hot, all_quads, (((0,), (0,)), ((), ())), preferred_element_type=jnp.float32
    )
    new_part = rebuild(summed, weight_tiles, keep_rows)
    new_full = lax.all_gather(new_part, "tok", axis=0, tiled=True)
    values = forward(next_inputs, new_full)
    return (values, new_momentum[None])


def solution(mesh):
    return jax.shard_map(
        local,
        mesh=mesh,
        in_specs=(
            P(("replica", "tok"), None),
            P(("replica", "tok"), None),
            P(("replica", "tok"), None),
            P("tok", None),
            P("replica", "tok", None),
            P("replica", "tok", None),
            P("replica", "tok"),
        ),
        out_specs=(P(("replica", "tok"), None), P("replica", "tok", None)),
        check_vma=False,
    )
```

profile of v0, /device:TPU:0, one launch (start us, length us, event | category | flops | bytes accessed | tf_op | source)
XLA Modules:
  0.0 222.4 jit_solution(13789088672530609271)
XLA Ops:
  7.2 1.3 copy-done
  8.5 3.5 %multiply_convert_fusion = bf16[2880,512]{1,0:T(8,128)(2,1)} fusion(bf16[256,2880]{0,1:T(8,128)(2,1)S(1)} %copy-done, bf16[256,512]{1,0:T(8,128)(2,1)} %param.8), kind=kOutput, calls=%fused_computation.2 | convolution fusion | flops 757923840 | bytes 4685824 | tf_op jit(solution)/shard_map/dot_general | solution.py:51
  12.1 8.4 %convert_element_type.37 = bf16[45,64,8,64]{3,2,1,0:T(8,128)(2,1)} reshape(bf16[2880,512]{1,0:T(8,128)(2,1)} %multiply_convert_fusion) | data formatting | bytes 5898240 | tf_op jit(solution)/shard_map/convert_element_type | solution.py:59
  20.5 7.0 %copy.22 = bf16[45,8,64,64]{3,2,1,0:T(8,128)(2,1)} copy(bf16[45,8,64,64]{3,1,2,0:T(8,128)(2,1)} %bitcast.59) | data formatting | bytes 5898240 | tf_op jit(solution)/shard_map/convert_element_type | solution.py:59
  27.5 8.7 %convert_element_type.39 = bf16[360,4096]{1,0:T(8,128)(2,1)} reshape(bf16[45,8,64,64]{3,2,1,0:T(8,128)(2,1)} %copy.22) | data formatting | bytes 5898240 | tf_op jit(solution)/shard_map/convert_element_type | solution.py:59
  36.2 61.9 %fusion = bf16[96,4096]{1,0:T(8,128)(2,1)S(1)} fusion(bf16[360,4096]{1,0:T(8,128)(2,1)} %convert_element_type.39), kind=kCustom, calls=%all-reduce-scatter | all-reduce-scatter fusion | flops 1572865 | bytes 3736064
  98.2 1.7 collective-permute-start
  100.6 0.6 dynamic-slice
  102.0 0.6 dynamic-slice.5
  103.2 8.0 %all-reduce = s32[64]{0:T(128)S(1)} all-reduce(s32[64]{0:T(128)S(1)} %fusion.39), channel_id=1, replica_groups=mesh['replica'=8,'tok'=4] {'replica'}, use_global_device_ids=true, to_apply=%add | all-reduce | flops 64 | bytes 512
  111.3 5.8 %concatenate = bf16[114,4096]{1,0:T(8,128)(2,1)} concatenate(bf16[18,4096]{1,0:T(8,128)(2,1)S(1)} %collective-permute-done, bf16[96,4096]{1,0:T(8,128)(2,1)S(1)} %fusion), dimensions={0} | concatenate | bytes 1867776
  117.1 2.9 %bitcast_add_fusion = f32[90,4096]{1,0:T(8,128)S(1)} fusion(f32[1,90,4096]{2,0,1:T(1,128)} %param.11, bf16[114,4096]{1,0:T(8,128)(2,1)} %concatenate, u32[]{:S(6)} %subtract), kind=kLoop, calls=%fused_computation.4 | loop fusion | flops 1105920 | bytes 3686404 | tf_op jit(solution)/shard_map/add | solution.py:61
  119.9 0.6 gather_fusion
  120.5 0.1 gather.7
  120.6 0.4 fusion.7
  121.0 0.3 fusion.2
  121.3 0.1 reshape.90
  121.5 8.7 %all_gather.10 = bf16[64,1024]{1,0:T(8,128)(2,1)S(1)} all-gather(bf16[8,1024]{1,0:T(8,128)(2,1)S(1)} %reshape.90), channel_id=1, replica_groups=mesh['replica'=8,'tok'=4] {'replica'}, dimensions={0}, use_global_device_ids=true | all-gather | bytes 147456 | tf_op jit(solution)/shard_map/all_gather | solution.py:75
  130.2 0.3 fusion.11
  130.5 1.4 fusion.5
  131.9 3.9 %convolution_multiply_fusion = f32[90,64,64]{0,2,1:T(8,128)} fusion(f32[90,32,64]{0,2,1:T(8,128)S(1)} %fusion.5, f32[32]{0:T(128)S(1)} %compare_select_fusion.2, f32[64]{0:T(128)S(1)} %add_multiply_fusion), kind=kOutput, calls=%fused_computation.3 | convolution fusion | flops 141932544 | bytes 2212224 | tf_op jit(solution)/shard_map/ua,tuv,vb->tab/dot_general | solution.py:23
  135.8 2.8 %copy.26 = f32[90,4096]{1,0:T(8,128)} copy(f32[90,4096]{0,1:T(8,128)} %bitcast.61) | data formatting | bytes 2949120 | tf_op jit(solution)/shard_map/mul | solution.py:26
  138.6 2.6 %fusion.4 = bf16[1,90,4096]{2,1,0:T(8,128)(2,1)} fusion(f32[90,4096]{1,0:T(8,128)} %copy.26, bf16[90,4096]{1,0:T(8,128)(2,1)} %param.10), kind=kLoop, calls=%fused_computation.13 | loop fusion | flops 1105920 | bytes 2949120
  141.3 0.3 fusion.13
  141.6 0.6 convolution_negate_fusion
  142.2 0.1 reshape.106
  142.3 1.3 scatter_fusion
  143.7 2.6 %copy.30 = f32[1,90,4096]{2,0,1:T(1,128)} copy(f32[1,90,4096]{2,1,0:T(8,128)S(1)} %bitcast.60) | data formatting | bytes 2949120
  146.3 55.8 %all-gather.3.cloned.1.call-done = bf16[4,90,4096]{2,1,0:T(8,128)(2,1)} async-done(((bf16[1,90,4096]{2,1,0:T(8,128)(2,1)}), bf16[4,90,4096]{2,1,0:T(8,128)(2,1)}) %all-gather.3.cloned.1.call-update) | async-done | bytes 2949136 | tf_op jit(solution)/shard_map/all_gather | solution.py:83
  202.1 8.2 %reshape.92 = bf16[45,8,64,64]{3,2,1,0:T(8,128)(2,1)} reshape(bf16[4,90,4096]{2,1,0:T(8,128)(2,1)} %all-gather.3.cloned.1.call-done) | data formatting | bytes 5898240 | tf_op jit(solution)/shard_map/reshape | solution.py:36
  210.2 4.4 %fusion.1 = bf16[8,64,256]{2,1,0:T(8,128)(2,1)S(1)} fusion(bf16[45,8,64,64]{3,2,1,0:T(8,128)(2,1)} %reshape.92, bf16[256,45,64,1]{0,2,3,1:T(8,128)(2,1)S(1)} %bitcast.63), kind=kOutput, calls=%fused_computation.8 | convolution fusion | flops 755105792 | bytes 4685824 | tf_op jit(solution)/shard_map/tra,rcab->tcb/dot_general | solution.py:37
  214.7 0.8 copy.29
  (21 shorter events, 0.3 us)
Async XLA Ops:
  7.2 1.4 copy-start
  7.2 194.9 %all-gather.3.cloned.1.call-start = ((), (), s32[]{:S(2)}) async-start(), calls=%async_computation | async-start | bytes 3932160 | tf_op jit(solution)/shard_map/all_gather | solution.py:83
  36.2 63.7 %copy-start.3 = (s32[1,1,8]{2,1,0:T(1,128)S(1)}, s32[1,1,8]{2,1,0:T(1,128)}, u32[]{:S(2)}) copy-start(s32[1,1,8]{2,1,0:T(1,128)} %param.12) | copy-start | bytes 100
  36.2 64.4 %copy-start.4 = (u32[32]{0:T(128)S(1)}, u32[32]{0:T(128)}, u32[]{:S(2)}) copy-start(u32[32]{0:T(128)} %constant.48) | copy-start | bytes 388
  36.2 65.8 %copy-start.2 = (u32[32]{0:T(128)S(1)}, u32[32]{0:T(128)}, u32[]{:S(2)}) copy-start(u32[32]{0:T(128)} %constant.54) | copy-start | bytes 388
  98.2 13.1 %collective-permute-start = (bf16[18,4096]{1,0:T(8,128)(2,1)S(1)}, bf16[18,4096]{1,0:T(8,128)(2,1)S(1)}, u32[]{:S(2)}, u32[]{:S(2)}) collective-permute-start(bf16[18,4096]{1,0:T(8,128)(2,1)S(1)} %slice.2), channel_id=1, source_target_pairs={{0,1},{1,2},{2,3},{4,5},{5,6},{6,7},{8,9},{9,10},{10,11},{12,13},{... | collective-permute-start | bytes 442376
  146.3 64.0 %copy-start.1 = (bf16[256,2880]{0,1:T(8,128)(2,1)S(1)}, bf16[256,2880]{0,1:T(8,128)(2,1)}, u32[]{:S(2)}) copy-start(bf16[256,2880]{0,1:T(8,128)(2,1)} %param.9) | copy-start | bytes 4423684
Sparse Core Ops, SparseCore 0:
  141.4 60.6 all-gather.2
where the time goes:
time: 224 us; the launch traced here: 222 us
  blocking collectives  78.7 us (35%)
  waiting for transfers between devices  55.8 us (25%)
  local copies, waits for them, and re-layouts  47.9 us (21%)
  between operations  16.2 us (7%)
  matrix products  15.1 us (7%)
  other arithmetic  6.99 us (3%)
    unnamed x2, blocking collectives  69.9 us
    all_gather x1, waiting for transfers between devices, local(): new_full = lax.all_gather(new_part, 'tok', axis=0, tiled=True)  55.8 us
    convert_element_type x3, local copies, waits for them, and re-layouts, local(): tiled.astype(jnp.bfloat16)  24.1 us
    unnamed x17, local copies, waits for them, and re-layouts  11.9 us
    all_gather x1, blocking collectives, local(): lax.all_gather(flat_quads, 'replica', axis=0, tiled=True)  8.73 us
    reshape x1, local copies, waits for them, and re-layouts, forward(): matrix = new_tiles.reshape(row_tiles, col_tiles, TILE, TILE)  8.17 us
    dot_general x2, matrix products, rebuild(): jnp.einsum('ua,tuv,vb->tab', keep_rows, quads, keep_rows, precision=lax.P...  5.25 us
  transfers between devices with their start and end apart: 2, of which 1 were waited for; matrix products, arithmetic and copies ran while one was open for 3% of the time, Pallas kernels for 0%

commit v1 on v0

--- a/solution.py
+++ b/solution.py
@@ -8,6 +8,24 @@
 KEEP = 32
 momentum_decay = 0.9
 step_size = 0.01
+
+
+def joined_along(parts, dim):
+    parts = jnp.moveaxis(parts, 0, dim)
+    dims = parts.shape
+    return parts.reshape(*dims[:dim], dims[dim] * dims[dim + 1], *dims[dim + 2 :])
+
+
+def collected_by_bits(value, axis):
+    size = lax.axis_size(axis)
+    blocks = value[None]
+    for level in range(size.bit_length() - 1):
+        distance = 1 << level
+        other = lax.ppermute(blocks, axis, [(i, i ^ distance) for i in range(size)])
+        both = jnp.stack([blocks, other])
+        upper = lax.axis_index(axis) >> level & 1
+        blocks = jnp.where(upper == 0, both, both[::-1]).reshape(-1, *value.shape)
+    return blocks
 
 
 def cosine_rows(count):
@@ -80,7 +98,7 @@
         one_hot, all_quads, (((0,), (0,)), ((), ())), preferred_element_type=jnp.float32
     )
     new_part = rebuild(summed, weight_tiles, keep_rows)
-    new_full = lax.all_gather(new_part, "tok", axis=0, tiled=True)
+    new_full = joined_along(collected_by_bits(new_part, "tok"), 0)
     values = forward(next_inputs, new_full)
     return (values, new_momentum[None])
 

time: 224 us -> 247 us (1.10)
  waiting for transfers between devices: 55.8 us -> 80.5 us
  between operations: 16.2 us -> 2.78 us
  other arithmetic: 6.99 us -> 13.5 us
  local copies, waits for them, and re-layouts: 47.9 us -> 53 us
    ppermute x0 -> x2, waiting for transfers between devices: none -> 80.5 us  [collected_by_bits(): other = lax.ppermute(blocks, axis, [(i, i ^ distance) for i in range(size)])]
    all_gather x1 -> x0, waiting for transfers between devices: 55.8 us -> none  [local(): new_full = lax.all_gather(new_part, 'tok', axis=0, tiled=True)]
    another operation x0 -> x1, local copies, waits for them, and re-layouts: none -> 8.29 us  [forward(): matrix = new_tiles.reshape(row_tiles, col_tiles, TILE, TILE)]
    another operation x0 -> x4, other arithmetic: none -> 6.39 us  [collected_by_bits(): both = jnp.stack([blocks, other])]
    reshape x1, local copies, waits for them, and re-layouts: 8.17 us -> 2.65 us  [collected_by_bits(): blocks = jnp.where(upper == 0, both, both[::-1]).reshape(-1, *value.shape)]
    unnamed x2 -> x1, other arithmetic: 2.74 us -> 0.1 us
    select_n x0 -> x1, other arithmetic: none -> 2.5 us  [collected_by_bits(): blocks = jnp.where(upper == 0, both, both[::-1]).reshape(-1, *value.shape)]
    unnamed x17 -> x19, local copies, waits for them, and re-layouts: 11.9 us -> 11.9 us
  transfers between devices with their start and end apart: 2 -> 3, of which waited for: 1 -> 2; matrix products, arithmetic and copies ran while one was open for 3% -> 3% of each run, Pallas kernels for 0% -> 0%
where the time goes in v1:
time: 247 us; the launch traced here: 246 us
  waiting for transfers between devices  80.5 us (33%)
  blocking collectives  78.7 us (32%)
  local copies, waits for them, and re-layouts  53 us (21%)
  matrix products  15.1 us (6%)
  other arithmetic  13.5 us (5%)
  between operations  2.78 us (1%)
    ppermute x2, waiting for transfers between devices, collected_by_bits(): other = lax.ppermute(blocks, axis, [(i, i ^ distance) for i in range(size)])  80.5 us
    unnamed x2, blocking collectives  69.9 us
    convert_element_type x3, local copies, waits for them, and re-layouts, local(): tiled.astype(jnp.bfloat16)  24.1 us
    unnamed x19, local copies, waits for them, and re-layouts  11.9 us
    all_gather x1, blocking collectives, local(): lax.all_gather(flat_quads, 'replica', axis=0, tiled=True)  8.73 us
    another operation x1, local copies, waits for them, and re-layouts, forward(): matrix = new_tiles.reshape(row_tiles, col_tiles, TILE, TILE)  8.29 us
    another operation x4, other arithmetic, collected_by_bits(): both = jnp.stack([blocks, other])  6.39 us
    dot_general x2, matrix products, rebuild(): jnp.einsum('ua,tuv,vb->tab', keep_rows, quads, keep_rows, precision=lax.P...  5.24 us
  transfers between devices with their start and end apart: 3, of which 2 were waited for; matrix products, arithmetic and copies ran while one was open for 3% of the time, Pallas kernels for 0%

profile of v1, /device:TPU:0, one launch (start us, length us, event | category | flops | bytes accessed | tf_op | source)
XLA Modules:
  0.0 245.8 jit_solution(10565418690630978139)
XLA Ops:
  0.6 1.4 copy-done
  2.0 3.5 %multiply_convert_fusion = bf16[2880,512]{1,0:T(8,128)(2,1)} fusion(bf16[256,2880]{0,1:T(8,128)(2,1)S(1)} %copy-done, bf16[256,512]{1,0:T(8,128)(2,1)} %param.8), kind=kOutput, calls=%fused_computation.2 | convolution fusion | flops 757923840 | bytes 4685824 | tf_op jit(solution)/shard_map/dot_general | solution.py:69
  5.5 8.4 %convert_element_type.37 = bf16[45,64,8,64]{3,2,1,0:T(8,128)(2,1)} reshape(bf16[2880,512]{1,0:T(8,128)(2,1)} %multiply_convert_fusion) | data formatting | bytes 5898240 | tf_op jit(solution)/shard_map/convert_element_type | solution.py:77
  13.9 7.0 %copy.35 = bf16[45,8,64,64]{3,2,1,0:T(8,128)(2,1)} copy(bf16[45,8,64,64]{3,1,2,0:T(8,128)(2,1)} %bitcast.69) | data formatting | bytes 5898240 | tf_op jit(solution)/shard_map/convert_element_type | solution.py:77
  20.9 8.7 %convert_element_type.39 = bf16[360,4096]{1,0:T(8,128)(2,1)} reshape(bf16[45,8,64,64]{3,2,1,0:T(8,128)(2,1)} %copy.35) | data formatting | bytes 5898240 | tf_op jit(solution)/shard_map/convert_element_type | solution.py:77
  29.7 61.9 %fusion = bf16[96,4096]{1,0:T(8,128)(2,1)S(1)} fusion(bf16[360,4096]{1,0:T(8,128)(2,1)} %convert_element_type.39), kind=kCustom, calls=%all-reduce-scatter | all-reduce-scatter fusion | flops 1572865 | bytes 3736064
  91.6 1.7 collective-permute-start.2
  94.1 0.6 dynamic-slice
  95.4 0.6 dynamic-slice.5
  96.7 8.0 %all-reduce = s32[64]{0:T(128)S(1)} all-reduce(s32[64]{0:T(128)S(1)} %fusion.40), channel_id=1, replica_groups=mesh['replica'=8,'tok'=4] {'replica'}, use_global_device_ids=true, to_apply=%add | all-reduce | flops 64 | bytes 512
  104.7 5.8 %concatenate = bf16[114,4096]{1,0:T(8,128)(2,1)} concatenate(bf16[18,4096]{1,0:T(8,128)(2,1)S(1)} %collective-permute-done.2, bf16[96,4096]{1,0:T(8,128)(2,1)S(1)} %fusion), dimensions={0} | concatenate | bytes 1867776
  110.5 2.9 %bitcast_add_fusion = f32[90,4096]{1,0:T(8,128)S(1)} fusion(f32[1,90,4096]{2,0,1:T(1,128)} %param.11, bf16[114,4096]{1,0:T(8,128)(2,1)} %concatenate, u32[]{:S(6)} %subtract), kind=kLoop, calls=%fused_computation.8 | loop fusion | flops 1105920 | bytes 3686404 | tf_op jit(solution)/shard_map/add | solution.py:79
  113.4 0.6 gather_fusion
  114.1 0.4 fusion.8
  114.9 8.7 %all_gather.7 = bf16[64,1024]{1,0:T(8,128)(2,1)S(1)} all-gather(bf16[8,1024]{1,0:T(8,128)(2,1)S(1)} %reshape.90), channel_id=1, replica_groups=mesh['replica'=8,'tok'=4] {'replica'}, dimensions={0}, use_global_device_ids=true | all-gather | bytes 147456 | tf_op jit(solution)/shard_map/all_gather | solution.py:93
  124.0 1.4 fusion.6
  125.3 3.9 %convolution_multiply_fusion = f32[90,64,64]{0,2,1:T(8,128)} fusion(f32[90,32,64]{0,2,1:T(8,128)S(1)} %fusion.6, f32[32]{0:T(128)S(1)} %compare_select_fusion.2, f32[64]{0:T(128)S(1)} %add_multiply_fusion), kind=kOutput, calls=%fused_computation.6 | convolution fusion | flops 141932544 | bytes 2212224 | tf_op jit(solution)/shard_map/ua,tuv,vb->tab/dot_general | solution.py:41
  129.2 2.9 %copy.39 = f32[90,4096]{1,0:T(8,128)} copy(f32[90,4096]{0,1:T(8,128)} %bitcast.71) | data formatting | bytes 2949120 | tf_op jit(solution)/shard_map/mul | solution.py:44
  132.1 3.0 %fusion.49 = (bf16[1,1,90,4096]{3,2,1,0:T(8,128)(2,1)}, bf16[1,90,4096]{2,1,0:T(8,128)(2,1)}) fusion(f32[90,4096]{1,0:T(8,128)} %copy.39, bf16[90,4096]{1,0:T(8,128)(2,1)} %param.10), kind=kLoop, calls=%fused_computation.73 | loop fusion | flops 1105920 | bytes 3686400 | tf_op jit(solution)/shard_map/stack;broadcast_in_dim | solution.py:25
  135.4 19.8 %collective-permute-done = bf16[1,90,4096]{2,1,0:T(8,128)(2,1)} collective-permute-done((bf16[1,90,4096]{2,1,0:T(8,128)(2,1)}, bf16[1,90,4096]{2,1,0:T(8,128)(2,1)}, u32[]{:S(2)}, u32[]{:S(2)}) %collective-permute-start) | collective-permute-done | bytes 737312 | tf_op jit(solution)/shard_map/ppermute | solution.py:24
  155.2 1.5 pad_maximum_fusion.1
  156.7 1.6 fusion.3
  158.3 2.7 %copy.40 = bf16[2,90,4096]{2,0,1:T(2,128)(2,1)} copy(bf16[2,90,4096]{2,1,0:T(8,128)(2,1)S(1)} %get-tuple-element.13) | data formatting | bytes 2949120 | tf_op jit(solution)/shard_map/reshape | solution.py:27
  161.6 0.6 convolution_negate_fusion
  162.3 1.6 scatter_fusion
  163.9 2.6 %copy.45 = f32[1,90,4096]{2,0,1:T(1,128)} copy(f32[1,90,4096]{2,1,0:T(8,128)S(1)} %bitcast.70) | data formatting | bytes 2949120
  166.5 60.7 %collective-permute-done.1 = bf16[2,90,4096]{2,0,1:T(2,128)(2,1)} collective-permute-done((bf16[2,90,4096]{2,0,1:T(2,128)(2,1)}, bf16[2,90,4096]{2,0,1:T(2,128)(2,1)}, u32[]{:S(2)}, u32[]{:S(2)}) %collective-permute-start.1) | collective-permute-done | bytes 1474592 | tf_op jit(solution)/shard_map/ppermute | solution.py:24
  227.2 2.2 copy.58
  229.8 2.5 %reverse_select_fusion = bf16[2,2,90,4096]{3,2,1,0:T(8,128)(2,1)} fusion(bf16[2,2,90,4096]{3,2,1,0:T(8,128)(2,1)S(1)} %pad_maximum_fusion, pred[]{:T(512)S(6)} %eq.40), kind=kLoop, calls=%fused_computation.3 | loop fusion | flops 1474560 | bytes 5898241 | tf_op jit(solution)/shard_map/jit(_where)/select_n | solution.py:27
  232.3 8.3 %reshape_reshape_reshape.3 = bf16[45,8,64,64]{3,2,1,0:T(8,128)(2,1)} reshape(bf16[2,2,90,4096]{3,2,1,0:T(8,128)(2,1)} %reverse_select_fusion) | data formatting | bytes 5898240 | tf_op jit(solution)/shard_map/reshape;reshape;reshape | solution.py:54
  240.6 4.4 %fusion.1 = bf16[8,64,256]{2,1,0:T(8,128)(2,1)S(1)} fusion(bf16[45,8,64,64]{3,2,1,0:T(8,128)(2,1)} %reshape_reshape_reshape.3, bf16[256,45,64,1]{0,2,3,1:T(8,128)(2,1)S(1)} %bitcast.74), kind=kOutput, calls=%fused_computation.13 | convolution fusion | flops 755105792 | bytes 4685824 | tf_op jit(solution)/shard_map/tra,rcab->tcb/dot_general | solution.py:55
  245.0 0.8 copy.44
  (30 shorter events, 2.4 us)
Async XLA Ops:
  0.6 1.4 copy-start
  29.7 63.7 %copy-start.4 = (s32[1,1,8]{2,1,0:T(1,128)S(1)}, s32[1,1,8]{2,1,0:T(1,128)}, u32[]{:S(2)}) copy-start(s32[1,1,8]{2,1,0:T(1,128)} %param.12) | copy-start | bytes 100
  29.7 64.4 %copy-start.5 = (u32[32]{0:T(128)S(1)}, u32[32]{0:T(128)}, u32[]{:S(2)}) copy-start(u32[32]{0:T(128)} %constant.55) | copy-start | bytes 388
  29.7 65.8 %copy-start.3 = (u32[32]{0:T(128)S(1)}, u32[32]{0:T(128)}, u32[]{:S(2)}) copy-start(u32[32]{0:T(128)} %constant.61) | copy-start | bytes 388
  91.6 13.1 %collective-permute-start.2 = (bf16[18,4096]{1,0:T(8,128)(2,1)S(1)}, bf16[18,4096]{1,0:T(8,128)(2,1)S(1)}, u32[]{:S(2)}, u32[]{:S(2)}) collective-permute-start(bf16[18,4096]{1,0:T(8,128)(2,1)S(1)} %slice.2), channel_id=1, source_target_pairs={{0,1},{1,2},{2,3},{4,5},{5,6},{6,7},{8,9},{9,10},{10,11},{12,13},{... | collective-permute-start | bytes 442376
  135.1 20.1 %collective-permute-start = (bf16[1,90,4096]{2,1,0:T(8,128)(2,1)}, bf16[1,90,4096]{2,1,0:T(8,128)(2,1)}, u32[]{:S(2)}, u32[]{:S(2)}) collective-permute-start(bf16[1,90,4096]{2,1,0:T(8,128)(2,1)} %get-tuple-element.11), channel_id=1, source_target_pairs={{0,1},{1,0},{2,3},{3,2},{4,5},{5,4},{6,7},{7,6},{8,9},{9,8},{10,11... | collective-permute-start | bytes 2211848 | tf_op jit(solution)/shard_map/ppermute | solution.py:24
  160.9 66.3 %collective-permute-start.1 = (bf16[2,90,4096]{2,0,1:T(2,128)(2,1)}, bf16[2,90,4096]{2,0,1:T(2,128)(2,1)}, u32[]{:S(2)}, u32[]{:S(2)}) collective-permute-start(bf16[2,90,4096]{2,0,1:T(2,128)(2,1)} %copy.40), channel_id=1, source_target_pairs={{0,2},{1,3},{2,0},{3,1},{4,6},{5,7},{6,4},{7,5},{8,10},{9,11},{10,... | collective-permute-start | bytes 4423688 | tf_op jit(solution)/shard_map/ppermute | solution.py:24
  166.5 62.9 %copy-start.1 = (bf16[1,2,90,4096]{3,2,1,0:T(8,128)(2,1)S(1)}, bf16[1,2,90,4096]{3,2,1,0:T(8,128)(2,1)}, u32[]{:S(2)}) copy-start(bf16[1,2,90,4096]{3,2,1,0:T(8,128)(2,1)} %get-tuple-element.12) | copy-start | bytes 4423684
  232.3 8.3 %copy-start.2 = (bf16[256,2880]{0,1:T(8,128)(2,1)S(1)}, bf16[256,2880]{0,1:T(8,128)(2,1)}, u32[]{:S(2)}) copy-start(bf16[256,2880]{0,1:T(8,128)(2,1)} %param.9) | copy-start | bytes 4423684
